TPU v7x, 32 devices: a whole 2x2x4 slice. The times are simulated.
32 devices in a mesh: groups: 2 (over y), hist: 4 (over z), tower: 2 (over x), head: 2 (over core).
Axes of the slice: x: 2, y: 2, z: 4, core: 2. Of those that a mesh axis runs over, the one named last changes fastest.
Arguments:
- queries: bfloat16 [1024, 1024], P(('groups', 'hist', 'tower'), 'head'), parts along dimension 0, may hold values from -6 to 6
- hist_keys: bfloat16 [4, 1024, 1024], P('groups', 'hist', 'head'), parts along dimension 0, may hold values from -6 to 6
- hist_values: bfloat16 [4, 1024, 1024], P('groups', 'hist', 'head'), parts along dimension 0, may hold values from -6 to 6
- cand_user: int32 [1024], P(('groups', 'hist', 'tower')), parts along dimension 0, may hold values from 0 to 1
- time_bucket: int32 [4, 1024], P('groups', 'hist'), parts along dimension 0, may hold values from 0 to 127
- hist_len: int32 [4], P('groups'), parts along dimension 0, may hold values from 256 to 1024
- cand_gate: bfloat16 [1024, 1024], P(('groups', 'hist', 'tower'), 'head'), parts along dimension 0, may hold values from -6 to 6
- time_bias: float32 [128, 8], P(None, 'head'), may hold values from -4 to 4
- tower_in: bfloat16 [1024, 4096], P('head', 'tower'), may hold values from -0.1875 to 0.1875
- tower_bias: float32 [4096], P('tower'), may hold values from -4 to 4
- tower_out: float32 [4096], P('tower'), may hold values from -0.09375 to 0.09375
Outputs:
- cand_states: bfloat16 [1024, 1024], P(('groups', 'hist', 'tower'), 'head'), parts along dimension 0
- cand_scores: float32 [1024], P(('groups', 'hist', 'tower')), parts along dimension 0
There are 2 independent parts, one for each index of `groups`. A program takes and returns all parts, laid end to end along the dimension named above; an argument that names none is the same for every part. Nothing has to cross between parts.
All inputs are finite; a program needn't handle non-finite values.
Results may differ from a plain program's by a relative error of at most 0.017.
Values may be sent and summed in bfloat16 or wider, within the bound.
A program may use at most 64 MiB of HBM per device.

v0:
```python
import functools

import jax
import jax.numpy as jnp
from jax import lax
from jax.experimental import pallas as pl
from jax.experimental.pallas import tpu as pltpu
from jax.sharding import PartitionSpec as P

DH = 128
CHUNKS = 2
MESH = pl.DeviceIdType.MESH
F32 = jnp.float32
BF16 = jnp.bfloat16


def partner_of(me, step, count):
    if count & (count - 1):
        return lax.rem(me + step, count)
    other, bit = 0, 1
    while bit < count:
        mine = lax.rem(me // bit, 2)
        other = other + (1 - mine if step & bit else mine) * bit
        bit *= 2
    return other


def source_of(me, step, count):
    if count & (count - 1):
        return lax.rem(me + count - step, count)
    return partner_of(me, step, count)


def kernel(
    n_hist,
    n_tower,
    q_hbm,
    k_hbm,
    v_hbm,
    user_hbm,
    bucket_hbm,
    len_ref,
    gate_hbm,
    tbias_hbm,
    w_hbm,
    b_hbm,
    o_hbm,
    states_out,
    scores_out,
    q_own,
    q_all,
    u_all,
    k_buf,
    v_buf,
    bucket,
    gate,
    tbias,
    w_buf,
    b_buf,
    o_buf,
    share_out,
    share_in,
    stat_buf,
    state_buf,
    score_send,
    score_in,
    load_sem,
    ready,
    pass_send,
    q_send,
    q_recv,
    u_send,
    u_recv,
    share_send,
    share_recv,
    one_send,
    one_recv,
    state_send,
    state_recv,
    score_send_sem,
    score_recv,
):
    z = lax.axis_index("hist")
    x = lax.axis_index("tower")
    c = lax.axis_index("head")
    mate = 1 - c
    rows, feat = q_hbm.shape
    users, per_user, _ = k_hbm.shape
    hidden = b_buf.shape[1]
    total_feat = 2 * feat

    tower_peers = [(t, h) for t in range(n_tower) for h in range(2) if t or h]

    def tower_id(t, h):
        return {"tower": partner_of(x, t, n_tower), "head": mate if h else c}

    has_left, has_right = z > 0, z < n_hist - 1
    sides = ((has_left, z - 1), (has_right, z + 1))

    barrier = pltpu.get_barrier_semaphore()
    for exists, there in sides:

        @pl.when(exists)
        def _(there=there):
            pl.semaphore_signal(barrier, inc=1, device_id={"hist": there}, device_id_type=MESH)

    for t, h in tower_peers:
        pl.semaphore_signal(barrier, inc=1, device_id=tower_id(t, h), device_id_type=MESH)

    mine_cols = pl.ds(pl.multiple_of(c * hidden, 128), hidden)
    mate_cols = pl.ds(pl.multiple_of(mate * hidden, 128), hidden)
    loads = [
        pltpu.make_async_copy(src, dst, load_sem.at[i])
        for i, (src, dst) in enumerate(
            [
                (q_hbm, q_own),
                (user_hbm, u_all.at[z]),
                (bucket_hbm, bucket),
                (tbias_hbm, tbias),
                (k_hbm, k_buf),
                (v_hbm, v_buf),
                (gate_hbm, gate),
                (b_hbm.at[:, mine_cols], b_buf),
                (o_hbm.at[:, mine_cols], o_buf),
                (w_hbm.at[:, mine_cols], w_buf.at[c]),
            ]
        )
    ]
    for load in loads:
        load.start()

    neighbours = has_left.astype(jnp.int32) + has_right.astype(jnp.int32)
    pl.semaphore_wait(barrier, neighbours + len(tower_peers))

    def remote(src, dst, send, recv, device_id):
        return pltpu.make_async_remote_copy(
            src_ref=src,
            dst_ref=dst,
            send_sem=send,
            recv_sem=recv,
            device_id=device_id,
            device_id_type=MESH,
        )

    chunks = q_all.shape[1]
    width = feat // chunks

    def query_copy(there, chunk):
        return remote(
            q_hbm.at[:, chunk * width : (chunk + 1) * width],
            q_all.at[z, chunk],
            q_send.at[there, chunk],
            q_recv.at[z, chunk],
            {"hist": there},
        )

    def user_copy(there):
        return remote(user_hbm, u_all.at[z], u_send.at[there], u_recv.at[z], {"hist": there})

    def each_other(action):
        for distance in range(1, n_hist):
            for sign, behind in ((-1, has_right), (1, has_left)):
                there = z + sign * distance
                pl.when((there >= 0) & (there < n_hist))(
                    functools.partial(action, distance, there, z - sign, behind)
                )

    def goes_direct(distance, behind):
        return jnp.logical_not(behind) if distance == 2 else z >= 0

    passes = (
        ((z >= 2) & (z + 1 < n_hist), z - 1, z + 1),
        ((z >= 1) & (z + 2 < n_hist), z + 1, z - 1),
    )

    def pass_copy(way, block, there, chunk):
        return remote(
            q_all.at[block, chunk],
            q_all.at[block, chunk],
            pass_send.at[way, chunk],
            q_recv.at[block, chunk],
            {"hist": there},
        )

    def send_queries(distance, there, back, behind):
        if distance > 1:
            pl.semaphore_wait(ready.at[there], 1)

        @pl.when(behind)
        def _():
            pl.semaphore_signal(
                ready.at[there], inc=1, device_id={"hist": back}, device_id_type=MESH
            )

        user_copy(there).start()

        @pl.when(goes_direct(distance, behind))
        def _():
            for chunk in range(chunks):
                query_copy(there, chunk).start()

    each_other(send_queries)
    sends = []
    w_copy = remote(
        w_hbm.at[:, mate_cols], w_buf.at[c], one_send.at[0], one_recv.at[0], {"head": mate}
    )
    w_copy.start()
    sends.append(w_copy)

    loads[2].wait()
    loads[3].wait()
    heads, bucket_count = tbias.shape
    half_scale = 0.5 * DH ** (-0.5)
    tb = tbias[...] * 0.5
    bias_rows, owner_rows = [], []
    for u in range(users):
        onehot = jnp.where(
            lax.broadcasted_iota(jnp.int32, (bucket_count, per_user), 0) == bucket[u : u + 1, :],
            1.0,
            0.0,
        ).astype(F32)
        bias_rows.append(
            lax.dot_general(
                tb,
                onehot,
                (((1,), (0,)), ((), ())),
                precision=lax.Precision.HIGHEST,
                preferred_element_type=F32,
            )
        )
        position = z * per_user + lax.broadcasted_iota(jnp.int32, (1, per_user), 1)
        owner_rows.append(jnp.where(position < len_ref[u], u, -1))
    bias = jnp.concatenate(bias_rows, axis=1)
    owner = jnp.concatenate(owner_rows, axis=1)
    events = users * per_user

    loads[0].wait()
    loads[1].wait()
    loads[4].wait()
    loads[5].wait()

    def live_of(index):
        user_col = jnp.broadcast_to(u_all[index], (128, rows)).T[:, :1]
        return jnp.where(user_col == owner, 1.0, 0.0).astype(F32)

    def attend(query, live, head):
        cols = slice(head * DH, (head + 1) * DH)
        s = lax.dot_general(
            query,
            k_buf[:, :, cols].reshape(events, DH),
            (((1,), (1,)), ((), ())),
            preferred_element_type=F32,
        )
        half = s * half_scale + bias[head : head + 1, :]
        weight = ((half + half * jnp.tanh(half)) * live).astype(BF16)
        return jnp.dot(
            weight, v_buf[:, :, cols].reshape(events, DH), preferred_element_type=F32
        ).astype(BF16)

    per_chunk = heads // chunks
    own_live = live_of(z)
    for head in range(heads):
        cols = slice((head % per_chunk) * DH, (head % per_chunk + 1) * DH)
        share_in[z, head // per_chunk, :, cols] = attend(
            q_own[:, head * DH : (head + 1) * DH], own_live, head
        )

    nearer = jnp.minimum(z, n_hist - 1 - z)

    def block_at(step):
        distance = (step + 1) // 2
        paired = z - distance if step % 2 else z + distance
        rest = jnp.where(z < n_hist - 1 - z, z + step - nearer, z - step + nearer)
        return jnp.where(step <= 2 * nearer, paired, rest)

    def users_arrive(block):
        remote(
            user_hbm, u_all.at[block], u_send.at[block], u_recv.at[block], {"hist": block}
        ).wait_recv()

    def arrive(block, chunk):
        remote(
            q_hbm.at[:, 0:width],
            q_all.at[block, chunk],
            q_send.at[block, chunk],
            q_recv.at[block, chunk],
            {"hist": block},
        ).wait_recv()

    def share_copy(step, chunk):
        return remote(
            share_out.at[step, chunk],
            share_in.at[z, chunk],
            share_send.at[step, chunk],
            share_recv.at[z, chunk],
            {"hist": block_at(step)},
        )

    for chunk in range(chunks):
        for way, (passing, block, there) in enumerate(passes):

            @pl.when(passing)
            def _(way=way, block=block, there=there, chunk=chunk):
                arrive(block, chunk)
                pass_copy(way, block, there, chunk).start()

    for step in range(1, n_hist):
        block = block_at(step)
        taken = (passes[0][0] & (block == z - 1)) | (passes[1][0] & (block == z + 1))
        for chunk in range(chunks):
            if chunk == 0:
                users_arrive(block)

            @pl.when(jnp.logical_not(taken))
            def _(block=block, chunk=chunk):
                arrive(block, chunk)

            if chunk == 0:
                live = live_of(block)
            for i in range(per_chunk):
                cols = slice(i * DH, (i + 1) * DH)
                share_out[step, chunk, :, cols] = attend(
                    q_all[block, chunk, :, cols], live, chunk * per_chunk + i
                )
            copy = share_copy(step, chunk)
            copy.start()
            sends.append(copy)

    for step in range(1, n_hist):
        src = block_at(step)
        for chunk in range(chunks):
            remote(
                share_out.at[step, chunk],
                share_in.at[src, chunk],
                share_send.at[step, chunk],
                share_recv.at[src, chunk],
                {"hist": src},
            ).wait_recv()
    parts = []
    for chunk in range(chunks):
        part = share_in[0, chunk].astype(F32)
        for s in range(1, n_hist):
            part = part + share_in[s, chunk].astype(F32)
        parts.append(part)
    attended = jnp.concatenate(parts, axis=1)

    row_sum = jnp.sum(attended, axis=1, keepdims=True)
    row_squares = jnp.sum(attended * attended, axis=1, keepdims=True)
    lane = lax.broadcasted_iota(jnp.int32, (rows, 128), 1)
    stat_buf[c] = jnp.where(lane == 0, row_sum, row_squares)
    stat_copy = remote(
        stat_buf.at[c], stat_buf.at[c], one_send.at[1], one_recv.at[1], {"head": mate}
    )
    stat_copy.start()
    sends.append(stat_copy)
    loads[6].wait()
    remote(
        stat_buf.at[mate], stat_buf.at[mate], one_send.at[1], one_recv.at[1], {"head": mate}
    ).wait_recv()
    stats = stat_buf[0] + stat_buf[1]
    row_mean = stats[:, 0:1] / total_feat
    row_var = stats[:, 1:2] / total_feat - row_mean * row_mean
    state_buf[x, c] = (
        (attended - row_mean) * lax.rsqrt(row_var + 1e-05) * gate[...].astype(F32)
    ).astype(BF16)

    for i, (t, h) in enumerate(tower_peers):
        copy = remote(
            state_buf.at[x, c],
            state_buf.at[x, c],
            state_send.at[i],
            state_recv.at[x, c],
            tower_id(t, h),
        )
        copy.start()
        sends.append(copy)
    states_out[...] = state_buf[x, c]

    loads[7].wait()
    loads[8].wait()
    loads[9].wait()
    remote(
        w_hbm.at[:, mate_cols], w_buf.at[mate], one_send.at[0], one_recv.at[0], {"head": mate}
    ).wait_recv()

    def wait_state(tower, head):
        remote(
            state_buf.at[tower, head],
            state_buf.at[tower, head],
            state_send.at[0],
            state_recv.at[tower, head],
            {"head": mate},
        ).wait_recv()

    def tower_scores(tower):
        pre = jnp.dot(state_buf[tower, 0], w_buf[0], preferred_element_type=F32)
        pre = pre + jnp.dot(state_buf[tower, 1], w_buf[1], preferred_element_type=F32)
        half = (pre + b_buf[...]) * 0.5
        part = (half + half * jnp.tanh(half)) * o_buf[...]
        acc = part[:, 0:128]
        for i in range(1, hidden // 128):
            acc = acc + part[:, i * 128 : (i + 1) * 128]
        return jnp.broadcast_to(jnp.sum(acc.T, axis=0, keepdims=True), (8, rows))

    wait_state(x, mate)
    own_scores = tower_scores(x)
    score_in[x, c] = own_scores
    copy = remote(
        score_in.at[x, c], score_in.at[x, c], score_send_sem.at[0], score_recv.at[x, c], {"head": mate}
    )
    copy.start()
    sends.append(copy)
    for t in range(1, n_tower):
        other = source_of(x, t, n_tower)
        wait_state(other, c)
        wait_state(other, mate)
        score_send[t] = tower_scores(other)
        for h in range(2):
            copy = remote(
                score_send.at[t],
                score_in.at[x, c],
                score_send_sem.at[2 * t + h],
                score_recv.at[x, c],
                {"tower": other, "head": mate if h else c},
            )
            copy.start()
            sends.append(copy)

    for t, h in tower_peers:
        tower, head = partner_of(x, t, n_tower), mate if h else c
        remote(
            score_in.at[tower, head],
            score_in.at[tower, head],
            score_send_sem.at[0],
            score_recv.at[tower, head],
            {"head": mate},
        ).wait_recv()
    total = score_in[0, 0] + score_in[0, 1]
    for t in range(1, n_tower):
        total = total + (score_in[t, 0] + score_in[t, 1])
    scores_out[...] = total[0:1, :]
    for copy in sends:
        copy.wait_send()

    def sent(distance, there, back, behind):
        user_copy(there).wait_send()

        @pl.when(goes_direct(distance, behind))
        def _():
            for chunk in range(chunks):
                query_copy(there, chunk).wait_send()

    each_other(sent)
    for way, (passing, block, there) in enumerate(passes):

        @pl.when(passing)
        def _(way=way, block=block, there=there):
            for chunk in range(chunks):
                pass_copy(way, block, there, chunk).wait_send()


def hand_over(states_in, scores_in, states_out, scores_out):
    states_out[...] = states_in[...]
    scores_out[...] = scores_in[...]


def local(
    queries,
    hist_keys,
    hist_values,
    cand_user,
    time_bucket,
    hist_len,
    cand_gate,
    time_bias,
    tower_in,
    tower_bias,
    tower_out,
    *,
    n_hist,
    n_tower,
):
    rows, feat = queries.shape
    hidden = tower_in.shape[1] // 2
    chunks = CHUNKS if (feat // DH) % CHUNKS == 0 else 1
    any_spec = pl.BlockSpec(memory_space=pl.ANY)
    vmem_spec = pl.BlockSpec(memory_space=pltpu.VMEM)
    dma = pltpu.SemaphoreType.DMA
    states, scores = pl.pallas_call(
        functools.partial(kernel, n_hist, n_tower),
        out_shape=(
            jax.ShapeDtypeStruct((rows, feat), BF16),
            jax.ShapeDtypeStruct((1, rows), F32),
        ),
        in_specs=[any_spec] * 5 + [pl.BlockSpec(memory_space=pltpu.SMEM)] + [any_spec] * 5,
        out_specs=(vmem_spec, vmem_spec),
        scratch_shapes=[
            pltpu.VMEM((rows, feat), BF16),
            pltpu.VMEM((n_hist, chunks, rows, feat // chunks), BF16),
            pltpu.VMEM((n_hist, 1, rows), jnp.int32),
            pltpu.VMEM(hist_keys.shape, BF16),
            pltpu.VMEM(hist_values.shape, BF16),
            pltpu.VMEM(time_bucket.shape, jnp.int32),
            pltpu.VMEM((rows, feat), BF16),
            pltpu.VMEM(time_bias.shape[::-1], F32),
            pltpu.VMEM((2, feat, hidden), BF16),
            pltpu.VMEM((1, hidden), F32),
            pltpu.VMEM((1, hidden), F32),
            pltpu.VMEM((n_hist, chunks, rows, feat // chunks), BF16),
            pltpu.VMEM((n_hist, chunks, rows, feat // chunks), BF16),
            pltpu.VMEM((2, rows, 128), F32),
            pltpu.VMEM((n_tower, 2, rows, feat), BF16),
            pltpu.VMEM((n_tower, 8, rows), F32),
            pltpu.VMEM((n_tower, 2, 8, rows), F32),
            dma((10,)),
            pltpu.SemaphoreType.REGULAR((n_hist,)),
            dma((2, chunks)),
            dma((n_hist, chunks)),
            dma((n_hist, chunks)),
            dma((n_hist,)),
            dma((n_hist,)),
            dma((n_hist, chunks)),
            dma((n_hist, chunks)),
            dma((2,)),
            dma((2,)),
            dma((2 * n_tower,)),
            dma((n_tower, 2)),
            dma((2 * n_tower,)),
            dma((n_tower, 2)),
        ],
        compiler_params=pltpu.CompilerParams(collective_id=0, has_side_effects=True),
    )(
        queries,
        hist_keys,
        hist_values,
        cand_user.reshape(1, rows),
        time_bucket,
        hist_len,
        cand_gate,
        time_bias.T,
        tower_in,
        tower_bias.reshape(1, -1),
        tower_out.reshape(1, -1),
    )
    states, scores = pl.pallas_call(
        hand_over,
        out_shape=(
            jax.ShapeDtypeStruct((rows, feat), BF16),
            jax.ShapeDtypeStruct((1, rows), F32),
        ),
        in_specs=[vmem_spec, vmem_spec],
        out_specs=(vmem_spec, vmem_spec),
    )(states, scores)
    return states, scores.reshape(rows)


def solution(mesh):
    return jax.shard_map(
        functools.partial(local, n_hist=mesh.shape["hist"], n_tower=mesh.shape["tower"]),
        mesh=mesh,
        in_specs=(
            P(("groups", "hist", "tower"), "head"),
            P("groups", "hist", "head"),
            P("groups", "hist", "head"),
            P(("groups", "hist", "tower")),
            P("groups", "hist"),
            P("groups"),
            P(("groups", "hist", "tower"), "head"),
            P(None, "head"),
            P("head", "tower"),
            P("tower"),
            P("tower"),
        ),
        out_specs=(P(("groups", "hist", "tower"), "head"), P(("groups", "hist", "tower"))),
        check_vma=False,
    )
```

profile of v0, /device:TPU:0, one launch (start us, length us, event | category | flops | bytes accessed | tf_op | source)
XLA Modules:
  0.0 30.7 jit_solution(6041263637141794632)
XLA Ops:
  0.6 28.6 %shard_map.122 = (bf16[64,512]{1,0:T(8,128)(2,1)}, f32[1,64]{1,0:T(1,128)}) custom-call(bf16[64,512]{1,0:T(8,128)(2,1)} %q_hbm.1, bf16[2,256,512]{2,1,0:T(8,128)(2,1)} %k_hbm.1, bf16[2,256,512]{2,1,0:T(8,128)(2,1)} %v_hbm.1, s32[1,64]{1,0:T(1,128)} %bitcast.8, s32[2,256]{1,0:T(2,128)} %bucket_hbm.1, s32[2]{0:T(128)} %len_ref.1, bf16[64,512]{1,0:T(8,128)(2,1)} %gate_hbm.1, ...), custom_call_target="tpu_custom_call" | custom-call | tf_op jit(solution)/shard_map/pallas_call | solution.py:489
  29.3 1.5 %shard_map.123 = (bf16[64,512]{1,0:T(8,128)(2,1)}, f32[1,64]{1,0:T(1,128)}) custom-call(bf16[64,512]{1,0:T(8,128)(2,1)} %get-tuple-element.6.states_in, f32[1,64]{1,0:T(1,128)} %get-tuple-element.7.scores_in), custom_call_target="tpu_custom_call" | custom-call | tf_op jit(solution)/shard_map/pallas_call | solution.py:545
where the time goes:
time: 30.9 us; the launch traced here: 30.7 us
  Pallas kernels  30.1 us (97%)
  between operations  0.64 us (2%)
    pallas_call x1, Pallas kernels, local(): pl.pallas_call(functools.partial(kernel, n_hist, n_tower), out_shape=(jax...  28.6 us
    pallas_call x1, Pallas kernels, local(): pl.pallas_call(hand_over, out_shape=(jax.ShapeDtypeStruct((rows, feat), B...  1.48 us

commit v1 on v0

--- a/solution.py
+++ b/solution.py
@@ -39,7 +39,7 @@
     v_hbm,
     user_hbm,
     bucket_hbm,
-    len_ref,
+    len_hbm,
     gate_hbm,
     tbias_hbm,
     w_hbm,
@@ -53,6 +53,7 @@
     k_buf,
     v_buf,
     bucket,
+    len_ref,
     gate,
     tbias,
     w_buf,
@@ -60,8 +61,7 @@
     o_buf,
     share_out,
     share_in,
-    stat_buf,
-    state_buf,
+    att_buf,
     score_send,
     score_in,
     load_sem,
@@ -73,10 +73,12 @@
     u_recv,
     share_send,
     share_recv,
-    one_send,
-    one_recv,
-    state_send,
-    state_recv,
+    w_send,
+    w_recv,
+    gate_send,
+    gate_recv,
+    att_send,
+    att_recv,
     score_send_sem,
     score_recv,
 ):
@@ -119,10 +121,11 @@
                 (tbias_hbm, tbias),
                 (k_hbm, k_buf),
                 (v_hbm, v_buf),
-                (gate_hbm, gate),
+                (gate_hbm, gate.at[x, c]),
                 (b_hbm.at[:, mine_cols], b_buf),
                 (o_hbm.at[:, mine_cols], o_buf),
                 (w_hbm.at[:, mine_cols], w_buf.at[c]),
+                (len_hbm, len_ref),
             ]
         )
     ]
@@ -202,13 +205,20 @@
     each_other(send_queries)
     sends = []
     w_copy = remote(
-        w_hbm.at[:, mate_cols], w_buf.at[c], one_send.at[0], one_recv.at[0], {"head": mate}
+        w_hbm.at[:, mate_cols], w_buf.at[c], w_send.at[0], w_recv.at[0], {"head": mate}
     )
     w_copy.start()
     sends.append(w_copy)
+    for i, (t, h) in enumerate(tower_peers):
+        copy = remote(
+            gate_hbm, gate.at[x, c], gate_send.at[i], gate_recv.at[x, c], tower_id(t, h)
+        )
+        copy.start()
+        sends.append(copy)
 
     loads[2].wait()
     loads[3].wait()
+    loads[10].wait()
     heads, bucket_count = tbias.shape
     half_scale = 0.5 * DH ** (-0.5)
     tb = tbias[...] * 0.5
@@ -229,7 +239,7 @@
             )
         )
         position = z * per_user + lax.broadcasted_iota(jnp.int32, (1, per_user), 1)
-        owner_rows.append(jnp.where(position < len_ref[u], u, -1))
+        owner_rows.append(jnp.where(position < len_ref[:, u : u + 1], u, -1))
     bias = jnp.concatenate(bias_rows, axis=1)
     owner = jnp.concatenate(owner_rows, axis=1)
     events = users * per_user
@@ -326,75 +336,74 @@
             copy.start()
             sends.append(copy)
 
-    for step in range(1, n_hist):
-        src = block_at(step)
-        for chunk in range(chunks):
-            remote(
-                share_out.at[step, chunk],
-                share_in.at[src, chunk],
-                share_send.at[step, chunk],
-                share_recv.at[src, chunk],
-                {"hist": src},
-            ).wait_recv()
-    parts = []
+    def share_arrives(src, chunk):
+        remote(
+            share_out.at[1, chunk],
+            share_in.at[src, chunk],
+            share_send.at[1, chunk],
+            share_recv.at[src, chunk],
+            {"hist": src},
+        ).wait_recv()
+
+    own = []
     for chunk in range(chunks):
+        for step in range(1, n_hist):
+            share_arrives(block_at(step), chunk)
         part = share_in[0, chunk].astype(F32)
         for s in range(1, n_hist):
             part = part + share_in[s, chunk].astype(F32)
-        parts.append(part)
-    attended = jnp.concatenate(parts, axis=1)
-
-    row_sum = jnp.sum(attended, axis=1, keepdims=True)
-    row_squares = jnp.sum(attended * attended, axis=1, keepdims=True)
-    lane = lax.broadcasted_iota(jnp.int32, (rows, 128), 1)
-    stat_buf[c] = jnp.where(lane == 0, row_sum, row_squares)
-    stat_copy = remote(
-        stat_buf.at[c], stat_buf.at[c], one_send.at[1], one_recv.at[1], {"head": mate}
-    )
-    stat_copy.start()
-    sends.append(stat_copy)
+        own.append(part)
+        att_buf[x, c, chunk] = part.astype(BF16)
+        for i, (t, h) in reversed(list(enumerate(tower_peers))):
+            copy = remote(
+                att_buf.at[x, c, chunk],
+                att_buf.at[x, c, chunk],
+                att_send.at[i, chunk],
+                att_recv.at[x, c, chunk],
+                tower_id(t, h),
+            )
+            copy.start()
+            sends.append(copy)
+
+    def half_arrives(tower, head):
+        remote(
+            gate_hbm, gate.at[tower, head], gate_send.at[0], gate_recv.at[tower, head], {"head": mate}
+        ).wait_recv()
+        for chunk in range(chunks):
+            remote(
+                att_buf.at[tower, head, chunk],
+                att_buf.at[tower, head, chunk],
+                att_send.at[0, chunk],
+                att_recv.at[tower, head, chunk],
+                {"head": mate},
+            ).wait_recv()
+
+    def half_of(tower, head):
+        return [att_buf[tower, head, chunk].astype(F32) for chunk in range(chunks)]
+
+    def normalised(pieces, gates):
+        every = [p for half in pieces for p in half]
+        row_sum = sum(jnp.sum(p, axis=1, keepdims=True) for p in every)
+        row_squares = sum(jnp.sum(p * p, axis=1, keepdims=True) for p in every)
+        row_mean = row_sum / total_feat
+        row_var = row_squares / total_feat - row_mean * row_mean
+        scale = lax.rsqrt(row_var + 1e-05)
+        return [
+            ((jnp.concatenate(half, axis=1) - row_mean) * scale * g.astype(F32)).astype(BF16)
+            for half, g in zip(pieces, gates)
+        ]
+
     loads[6].wait()
-    remote(
-        stat_buf.at[mate], stat_buf.at[mate], one_send.at[1], one_recv.at[1], {"head": mate}
-    ).wait_recv()
-    stats = stat_buf[0] + stat_buf[1]
-    row_mean = stats[:, 0:1] / total_feat
-    row_var = stats[:, 1:2] / total_feat - row_mean * row_mean
-    state_buf[x, c] = (
-        (attended - row_mean) * lax.rsqrt(row_var + 1e-05) * gate[...].astype(F32)
-    ).astype(BF16)
-
-    for i, (t, h) in enumerate(tower_peers):
-        copy = remote(
-            state_buf.at[x, c],
-            state_buf.at[x, c],
-            state_send.at[i],
-            state_recv.at[x, c],
-            tower_id(t, h),
-        )
-        copy.start()
-        sends.append(copy)
-    states_out[...] = state_buf[x, c]
-
     loads[7].wait()
     loads[8].wait()
     loads[9].wait()
     remote(
-        w_hbm.at[:, mate_cols], w_buf.at[mate], one_send.at[0], one_recv.at[0], {"head": mate}
+        w_hbm.at[:, mate_cols], w_buf.at[mate], w_send.at[0], w_recv.at[0], {"head": mate}
     ).wait_recv()
 
-    def wait_state(tower, head):
-        remote(
-            state_buf.at[tower, head],
-            state_buf.at[tower, head],
-            state_send.at[0],
-            state_recv.at[tower, head],
-            {"head": mate},
-        ).wait_recv()
-
-    def tower_scores(tower):
-        pre = jnp.dot(state_buf[tower, 0], w_buf[0], preferred_element_type=F32)
-        pre = pre + jnp.dot(state_buf[tower, 1], w_buf[1], preferred_element_type=F32)
+    def scores_of(first, first_w, second, second_w):
+        pre = jnp.dot(first, w_buf[first_w], preferred_element_type=F32)
+        pre = pre + jnp.dot(second, w_buf[second_w], preferred_element_type=F32)
         half = (pre + b_buf[...]) * 0.5
         part = (half + half * jnp.tanh(half)) * o_buf[...]
         acc = part[:, 0:128]
@@ -402,8 +411,10 @@
             acc = acc + part[:, i * 128 : (i + 1) * 128]
         return jnp.broadcast_to(jnp.sum(acc.T, axis=0, keepdims=True), (8, rows))
 
-    wait_state(x, mate)
-    own_scores = tower_scores(x)
+    half_arrives(x, mate)
+    mine, theirs = normalised([own, half_of(x, mate)], [gate[x, c], gate[x, mate]])
+    states_out[...] = mine
+    own_scores = scores_of(mine, c, theirs, mate)
     score_in[x, c] = own_scores
     copy = remote(
         score_in.at[x, c], score_in.at[x, c], score_send_sem.at[0], score_recv.at[x, c], {"head": mate}
@@ -412,9 +423,12 @@
     sends.append(copy)
     for t in range(1, n_tower):
         other = source_of(x, t, n_tower)
-        wait_state(other, c)
-        wait_state(other, mate)
-        score_send[t] = tower_scores(other)
+        half_arrives(other, c)
+        half_arrives(other, mate)
+        first, second = normalised(
+            [half_of(other, 0), half_of(other, 1)], [gate[other, 0], gate[other, 1]]
+        )
+        score_send[t] = scores_of(first, 0, second, 1)
         for h in range(2):
             copy = remote(
                 score_send.at[t],
@@ -489,10 +503,10 @@
     states, scores = pl.pallas_call(
         functools.partial(kernel, n_hist, n_tower),
         out_shape=(
-            jax.ShapeDtypeStruct((rows, feat), BF16),
-            jax.ShapeDtypeStruct((1, rows), F32),
+            pltpu.VMEM((rows, feat), BF16),
+            pltpu.VMEM((1, rows), F32),
         ),
-        in_specs=[any_spec] * 5 + [pl.BlockSpec(memory_space=pltpu.SMEM)] + [any_spec] * 5,
+        in_specs=[any_spec] * 11,
         out_specs=(vmem_spec, vmem_spec),
         scratch_shapes=[
             pltpu.VMEM((rows, feat), BF16),
@@ -501,18 +515,18 @@
             pltpu.VMEM(hist_keys.shape, BF16),
             pltpu.VMEM(hist_values.shape, BF16),
             pltpu.VMEM(time_bucket.shape, jnp.int32),
-            pltpu.VMEM((rows, feat), BF16),
+            pltpu.VMEM((1,) + hist_len.shape, jnp.int32),
+            pltpu.VMEM((n_tower, 2, rows, feat), BF16),
             pltpu.VMEM(time_bias.shape[::-1], F32),
             pltpu.VMEM((2, feat, hidden), BF16),
             pltpu.VMEM((1, hidden), F32),
             pltpu.VMEM((1, hidden), F32),
             pltpu.VMEM((n_hist, chunks, rows, feat // chunks), BF16),
             pltpu.VMEM((n_hist, chunks, rows, feat // chunks), BF16),
-            pltpu.VMEM((2, rows, 128), F32),
-            pltpu.VMEM((n_tower, 2, rows, feat), BF16),
+            pltpu.VMEM((n_tower, 2, chunks, rows, feat // chunks), BF16),
             pltpu.VMEM((n_tower, 8, rows), F32),
             pltpu.VMEM((n_tower, 2, 8, rows), F32),
-            dma((10,)),
+            dma((11,)),
             pltpu.SemaphoreType.REGULAR((n_hist,)),
             dma((2, chunks)),
             dma((n_hist, chunks)),
@@ -521,10 +535,12 @@
             dma((n_hist,)),
             dma((n_hist, chunks)),
             dma((n_hist, chunks)),
-            dma((2,)),
-            dma((2,)),
+            dma((1,)),
+            dma((1,)),
             dma((2 * n_tower,)),
             dma((n_tower, 2)),
+            dma((2 * n_tower, chunks)),
+            dma((n_tower, 2, chunks)),
             dma((2 * n_tower,)),
             dma((n_tower, 2)),
         ],
@@ -535,7 +551,7 @@
         hist_values,
         cand_user.reshape(1, rows),
         time_bucket,
-        hist_len,
+        hist_len.reshape(1, -1),
         cand_gate,
         time_bias.T,
         tower_in,
@@ -550,7 +566,10 @@
         ),
         in_specs=[vmem_spec, vmem_spec],
         out_specs=(vmem_spec, vmem_spec),
-    )(states, scores)
+    )(
+        pltpu.with_memory_space_constraint(states, pltpu.VMEM),
+        pltpu.with_memory_space_constraint(scores, pltpu.VMEM),
+    )
     return states, scores.reshape(rows)
 
 

time: 30.9 us -> 27 us (0.87)
  Pallas kernels: 30.1 us -> 26.2 us
    pallas_call x1, Pallas kernels: 28.6 us -> 25.6 us  [local(): pl.pallas_call(functools.partial(kernel, n_hist, n_tower), out_shape=(plt...]
    pallas_call x1, Pallas kernels: 1.48 us -> 0.64 us  [local(): pl.pallas_call(hand_over, out_shape=(jax.ShapeDtypeStruct((rows, feat), B...]
where the time goes in v1:
time: 27 us; the launch traced here: 26.8 us
  Pallas kernels  26.2 us (97%)
  between operations  0.64 us (2%)
    pallas_call x1, Pallas kernels, local(): pl.pallas_call(functools.partial(kernel, n_hist, n_tower), out_shape=(plt...  25.6 us
    pallas_call x1, Pallas kernels, local(): pl.pallas_call(hand_over, out_shape=(jax.ShapeDtypeStruct((rows, feat), B...  0.64 us

profile of v1, /device:TPU:0, one launch (start us, length us, event | category | flops | bytes accessed | tf_op | source)
XLA Modules:
  0.0 26.8 jit_solution(14650422921857523558)
XLA Ops:
  0.6 25.6 %shard_map.122 = (bf16[64,512]{1,0:T(8,128)(2,1)S(1)}, f32[1,64]{1,0:T(1,128)S(1)}) custom-call(bf16[64,512]{1,0:T(8,128)(2,1)} %q_hbm.1, bf16[2,256,512]{2,1,0:T(8,128)(2,1)} %k_hbm.1, bf16[2,256,512]{2,1,0:T(8,128)(2,1)} %v_hbm.1, s32[1,64]{1,0:T(1,128)} %bitcast.9, s32[2,256]{1,0:T(2,128)} %bucket_hbm.1, s32[1,2]{1,0:T(1,128)} %bitcast.10, ...), custom_call_target="tpu_custom_call" | custom-call | tf_op jit(solution)/shard_map/pallas_call | solution.py:503
  26.2 0.6 %shard_map.123 = (bf16[64,512]{1,0:T(8,128)(2,1)}, f32[1,64]{1,0:T(1,128)}) custom-call(bf16[64,512]{1,0:T(8,128)(2,1)S(1)} %get-tuple-element.6.states_in, f32[1,64]{1,0:T(1,128)S(1)} %get-tuple-element.7.scores_in), custom_call_target="tpu_custom_call" | custom-call | tf_op jit(solution)/shard_map/pallas_call | solution.py:561

commit v2 on v1

v2 whole, which is shorter than its diff:
```python
import functools

import jax
import jax.numpy as jnp
from jax import lax
from jax.experimental import pallas as pl
from jax.experimental.pallas import tpu as pltpu
from jax.sharding import PartitionSpec as P

DH = 128
CHUNKS = 2
MESH = pl.DeviceIdType.MESH
F32 = jnp.float32
BF16 = jnp.bfloat16


def partner_of(me, step, count):
    if count & (count - 1):
        return lax.rem(me + step, count)
    other, bit = 0, 1
    while bit < count:
        mine = lax.rem(me // bit, 2)
        other = other + (1 - mine if step & bit else mine) * bit
        bit *= 2
    return other


def source_of(me, step, count):
    if count & (count - 1):
        return lax.rem(me + count - step, count)
    return partner_of(me, step, count)


def relayed(block, at, count):
    return abs(block - at) == 2 and block not in (0, count - 1)


def order_of(at, count):
    def key(block):
        handed_on = 0 <= 2 * at - block < count and relayed(block, 2 * at - block, count)
        hops = at - block if block < at else at + 0.6 * (block - at)
        return not (handed_on and abs(at - block) == 1), relayed(block, at, count), hops

    return sorted((b for b in range(count) if b != at), key=key)


def pick(me, values):
    if all(v == values[0] for v in values):
        return values[0]
    chosen = jnp.int32(values[0])
    for i, v in enumerate(values[1:], 1):
        chosen = jnp.where(me == i, jnp.int32(v), chosen)
    return chosen


def when(condition):
    if isinstance(condition, bool):
        return (lambda body: body()) if condition else (lambda body: None)
    return pl.when(condition)


def kernel(
    n_hist,
    n_tower,
    q_hbm,
    k_hbm,
    v_hbm,
    user_hbm,
    bucket_hbm,
    len_hbm,
    gate_hbm,
    tbias_hbm,
    w_hbm,
    b_hbm,
    o_hbm,
    states_out,
    scores_out,
    q_all,
    u_all,
    k_buf,
    v_buf,
    bucket,
    len_ref,
    gate,
    tbias,
    w_buf,
    b_buf,
    o_buf,
    own_share,
    share_out,
    share_in,
    att_buf,
    score_send,
    score_in,
    load_sem,
    q_load,
    above,
    peers,
    pass_send,
    pass_user_send,
    q_send,
    q_recv,
    u_send,
    u_recv,
    share_send,
    share_recv,
    w_send,
    w_recv,
    gate_send,
    gate_recv,
    att_send,
    att_recv,
    score_send_sem,
    score_recv,
):
    z = lax.axis_index("hist")
    x = lax.axis_index("tower")
    c = lax.axis_index("head")
    mate = 1 - c
    rows, feat = q_hbm.shape
    users, per_user, _ = k_hbm.shape
    hidden = b_buf.shape[1]
    total_feat = 2 * feat
    chunks = q_all.shape[1]
    width = feat // chunks

    tower_peers = [(t, h) for t in range(n_tower) for h in range(2) if t or h]

    def tower_id(t, h):
        return {"tower": partner_of(x, t, n_tower), "head": mate if h else c}

    def rank_of(tower, head):
        return 2 * tower + 1 - head

    rank = rank_of(x, c)
    peer_ranks = [
        (t, h, rank_of(partner_of(x, t, n_tower), mate if h else c)) for t, h in tower_peers
    ]
    barrier = pltpu.get_barrier_semaphore()
    for t, h, other_rank in peer_ranks:

        @pl.when(other_rank > rank)
        def _(t=t, h=h):
            pl.semaphore_signal(barrier, inc=1, device_id=tower_id(t, h), device_id_type=MESH)

    has_left, has_right = z > 0, z < n_hist - 1

    mine_cols = pl.ds(pl.multiple_of(c * hidden, 128), hidden)
    mate_cols = pl.ds(pl.multiple_of(mate * hidden, 128), hidden)
    q_loads = [
        pltpu.make_async_copy(q_hbm.at[:, i * width : (i + 1) * width], q_all.at[z, i], q_load)
        for i in range(chunks)
    ]
    loads = [
        pltpu.make_async_copy(src, dst, load_sem.at[i])
        for i, (src, dst) in enumerate(
            [
                (user_hbm, u_all.at[z]),
                (bucket_hbm, bucket),
                (tbias_hbm, tbias),
                (len_hbm, len_ref),
                (k_hbm, k_buf),
                (v_hbm, v_buf),
                (gate_hbm, gate.at[x, c]),
                (b_hbm.at[:, mine_cols], b_buf),
                (o_hbm.at[:, mine_cols], o_buf),
                (w_hbm.at[:, mine_cols], w_buf.at[c]),
            ]
        )
    ]
    user_load, bucket_load, tbias_load, len_load, k_load, v_load, *late_loads = loads
    for load in q_loads + loads[:6]:
        load.start()

    awaited = rank + has_left.astype(jnp.int32)

    @pl.when(awaited > 0)
    def _():
        pl.semaphore_wait(barrier, awaited)

    @pl.when(has_right)
    def _():
        pl.semaphore_signal(barrier, inc=1, device_id={"hist": z + 1}, device_id_type=MESH)

    for distance in range(1, n_hist):

        @pl.when(z >= distance)
        def _(distance=distance):
            pl.semaphore_signal(
                above.at[z], inc=1, device_id={"hist": z - distance}, device_id_type=MESH
            )

    for t, h, other_rank in peer_ranks:

        @pl.when(other_rank < rank)
        def _(t=t, h=h):
            pl.semaphore_signal(peers, inc=1, device_id=tower_id(t, h), device_id_type=MESH)

    def remote(src, dst, send, recv, device_id):
        return pltpu.make_async_remote_copy(
            src_ref=src,
            dst_ref=dst,
            send_sem=send,
            recv_sem=recv,
            device_id=device_id,
            device_id_type=MESH,
        )

    def query_copy(there, chunk):
        return remote(
            q_all.at[z, chunk],
            q_all.at[z, chunk],
            q_send.at[there],
            q_recv.at[z, chunk],
            {"hist": there},
        )

    def user_copy(there):
        return remote(u_all.at[z], u_all.at[z], u_send.at[there], u_recv.at[z], {"hist": there})

    def send_queries(there):
        user_copy(there).start()
        for chunk in range(chunks):
            query_copy(there, chunk).start()

    def goes_direct(distance, sign):
        if distance != 2:
            return True
        return z == 0 if sign > 0 else z == n_hist - 1

    def send_down(distance):
        @pl.when(z >= distance)
        def _():
            when(goes_direct(distance, -1))(lambda: send_queries(z - distance))

    def send_up(distance, condition):
        @pl.when(condition)
        def _():
            pl.semaphore_wait(above.at[z + distance], 1)
            when(goes_direct(distance, 1))(lambda: send_queries(z + distance))

    user_load.wait()
    pltpu.make_async_copy(q_all.at[z], q_all.at[z], q_load).wait()
    for distance in range(n_hist - 1, 0, -1):
        send_down(distance)

    send_up(1, z < n_hist - 2)

    bucket_load.wait()
    tbias_load.wait()
    len_load.wait()
    heads, bucket_count = tbias.shape
    half_scale = 0.5 * DH ** (-0.5)
    tb = tbias[...] * 0.5
    bias_rows, owner_rows = [], []
    for u in range(users):
        onehot = jnp.where(
            lax.broadcasted_iota(jnp.int32, (bucket_count, per_user), 0) == bucket[u : u + 1, :],
            1.0,
            0.0,
        ).astype(F32)
        bias_rows.append(
            lax.dot_general(
                tb,
                onehot,
                (((1,), (0,)), ((), ())),
                precision=lax.Precision.HIGHEST,
                preferred_element_type=F32,
            )
        )
        position = z * per_user + lax.broadcasted_iota(jnp.int32, (1, per_user), 1)
        owner_rows.append(jnp.where(position < len_ref[:, u : u + 1], u, -1))
    bias = jnp.concatenate(bias_rows, axis=1)
    owner = jnp.concatenate(owner_rows, axis=1)
    events = users * per_user
    k_load.wait()
    v_load.wait()

    def live_of(index):
        user_col = jnp.broadcast_to(u_all[index], (128, rows)).T[:, :1]
        return jnp.where(user_col == owner, 1.0, 0.0).astype(F32)

    def attend(query, live, head):
        cols = slice(head * DH, (head + 1) * DH)
        s = lax.dot_general(
            query,
            k_buf[:, :, cols].reshape(events, DH),
            (((1,), (1,)), ((), ())),
            preferred_element_type=F32,
        )
        half = s * half_scale + bias[head : head + 1, :]
        weight = ((half + half * jnp.tanh(half)) * live).astype(BF16)
        return jnp.dot(
            weight, v_buf[:, :, cols].reshape(events, DH), preferred_element_type=F32
        )

    per_chunk = heads // chunks

    def share_of(block, live, chunk):
        parts = [
            attend(q_all[block, chunk, :, i * DH : (i + 1) * DH], live, chunk * per_chunk + i)
            for i in range(per_chunk)
        ]
        return jnp.concatenate(parts, axis=1) if per_chunk > 1 else parts[0]

    own_live = live_of(z)
    for chunk in range(chunks):
        own_share[chunk] = share_of(z, own_live, chunk)

    for load in late_loads:
        load.start()

    send_up(1, z == n_hist - 2)
    for distance in range(2, n_hist):
        send_up(distance, z + distance < n_hist)


    @pl.when(rank < 2 * n_tower - 1)
    def _():
        pl.semaphore_wait(peers, 2 * n_tower - 1 - rank)
    sends = []
    w_copy = remote(
        w_hbm.at[:, mate_cols], w_buf.at[c], w_send.at[0], w_recv.at[0], {"head": mate}
    )
    w_copy.start()
    sends.append(w_copy)
    for i, (t, h) in enumerate(tower_peers):
        copy = remote(
            gate_hbm, gate.at[x, c], gate_send.at[i], gate_recv.at[x, c], tower_id(t, h)
        )
        copy.start()
        sends.append(copy)

    def user_arrives(block):
        remote(
            u_all.at[block], u_all.at[block], u_send.at[0], u_recv.at[block], {"hist": block}
        ).wait_recv()

    def query_arrives(block, chunk):
        remote(
            q_all.at[block, chunk],
            q_all.at[block, chunk],
            q_send.at[0],
            q_recv.at[block, chunk],
            {"hist": block},
        ).wait_recv()

    def pass_copy(step, block, there, chunk):
        return remote(
            q_all.at[block, chunk],
            q_all.at[block, chunk],
            pass_send.at[step],
            q_recv.at[block, chunk],
            {"hist": there},
        )

    def pass_user(step, block, there):
        return remote(
            u_all.at[block],
            u_all.at[block],
            pass_user_send.at[step],
            u_recv.at[block],
            {"hist": there},
        )

    def share_copy(step, chunk):
        return remote(
            share_out.at[step, chunk],
            share_in.at[z, chunk],
            share_send.at[step],
            share_recv.at[z, chunk],
            {"hist": steps[step][0]},
        )

    def flag(values):
        chosen = pick(z, [int(v) for v in values])
        return bool(chosen) if isinstance(chosen, int) else chosen == 1

    orders = [order_of(i, n_hist) for i in range(n_hist)]
    steps = []
    for step in range(n_hist - 1):
        blocks = [order[step] for order in orders]
        onward = [2 * i - b for i, b in enumerate(blocks)]
        hands_on = [
            abs(i - b) == 1 and 0 <= e < n_hist and relayed(b, e, n_hist)
            for i, (b, e) in enumerate(zip(blocks, onward))
        ]
        targets = [e if on else 0 for e, on in zip(onward, hands_on)]
        steps.append((pick(z, blocks), flag(hands_on), pick(z, targets)))

    for step, (block, passing, there) in enumerate(steps):
        user_arrives(block)

        @when(passing)
        def _():
            pass_user(step, block, there).start()

        live = live_of(block)
        holding = not passing if isinstance(passing, bool) else jnp.logical_not(passing)

        @when(passing)
        def _():
            for chunk in range(chunks):
                query_arrives(block, chunk)
                pass_copy(step, block, there, chunk).start()

        for chunk in range(chunks):
            @when(holding)
            def _():
                query_arrives(block, chunk)

            share_out[step, chunk] = share_of(block, live, chunk).astype(BF16)
            share_copy(step, chunk).start()

    sources = [block for block, _, _ in steps]

    own = []
    for chunk in range(chunks):
        for src in sources:
            remote(
                share_out.at[0, chunk],
                share_in.at[src, chunk],
                share_send.at[0],
                share_recv.at[src, chunk],
                {"hist": src},
            ).wait_recv()
        part = own_share[chunk]
        for src in sources:
            part = part + share_in[src, chunk].astype(F32)
        own.append(part)
        att_buf[x, c, chunk] = part.astype(BF16)
        for i, (t, h) in reversed(list(enumerate(tower_peers))):
            copy = remote(
                att_buf.at[x, c, chunk],
                att_buf.at[x, c, chunk],
                att_send.at[i],
                att_recv.at[x, c, chunk],
                tower_id(t, h),
            )
            copy.start()

    def half_arrives(tower, head):
        remote(
            gate_hbm, gate.at[tower, head], gate_send.at[0], gate_recv.at[tower, head], {"head": mate}
        ).wait_recv()
        for chunk in range(chunks):
            remote(
                att_buf.at[tower, head, chunk],
                att_buf.at[tower, head, chunk],
                att_send.at[0],
                att_recv.at[tower, head, chunk],
                {"head": mate},
            ).wait_recv()

    def half_of(tower, head):
        return [att_buf[tower, head, chunk].astype(F32) for chunk in range(chunks)]

    def normalised(pieces, gates):
        every = [p for half in pieces for p in half]
        row_sum = sum(jnp.sum(p, axis=1, keepdims=True) for p in every)
        row_squares = sum(jnp.sum(p * p, axis=1, keepdims=True) for p in every)
        row_mean = row_sum / total_feat
        row_var = row_squares / total_feat - row_mean * row_mean
        scale = lax.rsqrt(row_var + 1e-05)
        return [
            ((jnp.concatenate(half, axis=1) - row_mean) * scale * g.astype(F32)).astype(BF16)
            for half, g in zip(pieces, gates)
        ]

    for load in late_loads:
        load.wait()
    remote(
        w_hbm.at[:, mate_cols], w_buf.at[mate], w_send.at[0], w_recv.at[0], {"head": mate}
    ).wait_recv()

    def scores_of(first, first_w, second, second_w):
        pre = jnp.dot(first, w_buf[first_w], preferred_element_type=F32)
        pre = pre + jnp.dot(second, w_buf[second_w], preferred_element_type=F32)
        half = (pre + b_buf[...]) * 0.5
        part = (half + half * jnp.tanh(half)) * o_buf[...]
        acc = part[:, 0:128]
        for i in range(1, hidden // 128):
            acc = acc + part[:, i * 128 : (i + 1) * 128]
        return jnp.sum(acc.T, axis=0, keepdims=True)

    half_arrives(x, mate)
    mine, theirs = normalised([own, half_of(x, mate)], [gate[x, c], gate[x, mate]])
    states_out[...] = mine
    own_scores = scores_of(mine, c, theirs, mate)
    score_in[x, c] = own_scores
    copy = remote(
        score_in.at[x, c], score_in.at[x, c], score_send_sem.at[0], score_recv.at[x, c], {"head": mate}
    )
    copy.start()
    sends.append(copy)
    for t in range(1, n_tower):
        other = source_of(x, t, n_tower)
        half_arrives(other, c)
        half_arrives(other, mate)
        first, second = normalised(
            [half_of(other, 0), half_of(other, 1)], [gate[other, 0], gate[other, 1]]
        )
        score_send[t] = scores_of(first, 0, second, 1)
        for h in range(2):
            copy = remote(
                score_send.at[t],
                score_in.at[x, c],
                score_send_sem.at[2 * t + h],
                score_recv.at[x, c],
                {"tower": other, "head": mate if h else c},
            )
            copy.start()
            sends.append(copy)

    for t, h in tower_peers:
        tower, head = partner_of(x, t, n_tower), mate if h else c
        remote(
            score_in.at[tower, head],
            score_in.at[tower, head],
            score_send_sem.at[0],
            score_recv.at[tower, head],
            {"head": mate},
        ).wait_recv()
    total = score_in[0, 0] + score_in[0, 1]
    for t in range(1, n_tower):
        total = total + (score_in[t, 0] + score_in[t, 1])
    scores_out[...] = total
    for copy in sends:
        copy.wait_send()
    for i, (t, h) in enumerate(tower_peers):
        remote(
            att_buf.at[x, c], att_buf.at[x, c], att_send.at[i], att_recv.at[x, c, 0], tower_id(t, h)
        ).wait_send()
    for step, (block, passing, there) in enumerate(steps):
        remote(
            share_out.at[step], share_in.at[z], share_send.at[step], share_recv.at[z, 0], {"hist": block}
        ).wait_send()

        @when(passing)
        def _():
            pass_user(step, block, there).wait_send()
            remote(
                q_all.at[block], q_all.at[block], pass_send.at[step], q_recv.at[block, 0], {"hist": there}
            ).wait_send()

    def sent(there):
        user_copy(there).wait_send()
        remote(
            q_all.at[z], q_all.at[z], q_send.at[there], q_recv.at[z, 0], {"hist": there}
        ).wait_send()

    for distance in range(1, n_hist):
        for sign, exists in ((-1, z >= distance), (1, z + distance < n_hist)):

            @pl.when(exists)
            def _(distance=distance, sign=sign):
                when(goes_direct(distance, sign))(lambda: sent(z + sign * distance))


def hand_over(states_in, scores_in, states_out, scores_out):
    states_out[...] = states_in[...]
    scores_out[...] = scores_in[...]


def local(
    queries,
    hist_keys,
    hist_values,
    cand_user,
    time_bucket,
    hist_len,
    cand_gate,
    time_bias,
    tower_in,
    tower_bias,
    tower_out,
    *,
    n_hist,
    n_tower,
):
    rows, feat = queries.shape
    hidden = tower_in.shape[1] // 2
    chunks = CHUNKS if (feat // DH) % CHUNKS == 0 else 1
    width = feat // chunks
    any_spec = pl.BlockSpec(memory_space=pl.ANY)
    vmem_spec = pl.BlockSpec(memory_space=pltpu.VMEM)
    dma = pltpu.SemaphoreType.DMA
    states, scores = pl.pallas_call(
        functools.partial(kernel, n_hist, n_tower),
        out_shape=(
            pltpu.VMEM((rows, feat), BF16),
            pltpu.VMEM((1, rows), F32),
        ),
        in_specs=[any_spec] * 11,
        out_specs=(vmem_spec, vmem_spec),
        scratch_shapes=[
            pltpu.VMEM((n_hist, chunks, rows, width), BF16),
            pltpu.VMEM((n_hist, 1, rows), jnp.int32),
            pltpu.VMEM(hist_keys.shape, BF16),
            pltpu.VMEM(hist_values.shape, BF16),
            pltpu.VMEM(time_bucket.shape, jnp.int32),
            pltpu.VMEM((1,) + hist_len.shape, jnp.int32),
            pltpu.VMEM((n_tower, 2, rows, feat), BF16),
            pltpu.VMEM(time_bias.shape[::-1], F32),
            pltpu.VMEM((2, feat, hidden), BF16),
            pltpu.VMEM((1, hidden), F32),
            pltpu.VMEM((1, hidden), F32),
            pltpu.VMEM((chunks, rows, width), F32),
            pltpu.VMEM((n_hist, chunks, rows, width), BF16),
            pltpu.VMEM((n_hist, chunks, rows, width), BF16),
            pltpu.VMEM((n_tower, 2, chunks, rows, width), BF16),
            pltpu.VMEM((n_tower, 1, rows), F32),
            pltpu.VMEM((n_tower, 2, 1, rows), F32),
            dma((10,)),
            dma,
            pltpu.SemaphoreType.REGULAR((n_hist,)),
            pltpu.SemaphoreType.REGULAR,
            dma((n_hist - 1,)),
            dma((n_hist - 1,)),
            dma((n_hist,)),
            dma((n_hist, chunks)),
            dma((n_hist,)),
            dma((n_hist,)),
            dma((n_hist - 1,)),
            dma((n_hist, chunks)),
            dma((1,)),
            dma((1,)),
            dma((2 * n_tower - 1,)),
            dma((n_tower, 2)),
            dma((2 * n_tower - 1,)),
            dma((n_tower, 2, chunks)),
            dma((2 * n_tower,)),
            dma((n_tower, 2)),
        ],
        compiler_params=pltpu.CompilerParams(collective_id=0, has_side_effects=True),
    )(
        queries,
        hist_keys,
        hist_values,
        cand_user.reshape(1, rows),
        time_bucket,
        hist_len.reshape(1, -1),
        cand_gate,
        time_bias.T,
        tower_in,
        tower_bias.reshape(1, -1),
        tower_out.reshape(1, -1),
    )
    states, scores = pl.pallas_call(
        hand_over,
        out_shape=(
            jax.ShapeDtypeStruct((rows, feat), BF16),
            jax.ShapeDtypeStruct((1, rows), F32),
        ),
        in_specs=[vmem_spec, vmem_spec],
        out_specs=(vmem_spec, vmem_spec),
    )(
        pltpu.with_memory_space_constraint(states, pltpu.VMEM),
        pltpu.with_memory_space_constraint(scores, pltpu.VMEM),
    )
    return states, scores.reshape(rows)


def solution(mesh):
    return jax.shard_map(
        functools.partial(local, n_hist=mesh.shape["hist"], n_tower=mesh.shape["tower"]),
        mesh=mesh,
        in_specs=(
            P(("groups", "hist", "tower"), "head"),
            P("groups", "hist", "head"),
            P("groups", "hist", "head"),
            P(("groups", "hist", "tower")),
            P("groups", "hist"),
            P("groups"),
            P(("groups", "hist", "tower"), "head"),
            P(None, "head"),
            P("head", "tower"),
            P("tower"),
            P("tower"),
        ),
        out_specs=(P(("groups", "hist", "tower"), "head"), P(("groups", "hist", "tower"))),
        check_vma=False,
    )
```

time: 27 us -> 25.6 us (0.948)
  Pallas kernels: 26.2 us -> 24.8 us
    pallas_call x1, Pallas kernels: 25.6 us -> 24.1 us  [local(): pl.pallas_call(functools.partial(kernel, n_hist, n_tower), out_shape=(plt...]
where the time goes in v2:
time: 25.6 us; the launch traced here: 25.4 us
  Pallas kernels  24.8 us (97%)
  between operations  0.64 us (2%)
    pallas_call x1, Pallas kernels, local(): pl.pallas_call(functools.partial(kernel, n_hist, n_tower), out_shape=(plt...  24.1 us
    pallas_call x1, Pallas kernels, local(): pl.pallas_call(hand_over, out_shape=(jax.ShapeDtypeStruct((rows, feat), B...  0.64 us

profile of v2, /device:TPU:0, one launch (start us, length us, event | category | flops | bytes accessed | tf_op | source)
XLA Modules:
  0.0 25.4 jit_solution(2688371501818619421)
XLA Ops:
  0.6 24.1 %shard_map.122 = (bf16[64,512]{1,0:T(8,128)(2,1)S(1)}, f32[1,64]{1,0:T(1,128)S(1)}) custom-call(bf16[64,512]{1,0:T(8,128)(2,1)} %q_hbm.1, bf16[2,256,512]{2,1,0:T(8,128)(2,1)} %k_hbm.1, bf16[2,256,512]{2,1,0:T(8,128)(2,1)} %v_hbm.1, s32[1,64]{1,0:T(1,128)} %bitcast.9, s32[2,256]{1,0:T(2,128)} %bucket_hbm.1, s32[1,2]{1,0:T(1,128)} %bitcast.10, ...), custom_call_target="tpu_custom_call" | custom-call | tf_op jit(solution)/shard_map/pallas_call | solution.py:588
  24.8 0.6 %shard_map.123 = (bf16[64,512]{1,0:T(8,128)(2,1)}, f32[1,64]{1,0:T(1,128)}) custom-call(bf16[64,512]{1,0:T(8,128)(2,1)S(1)} %get-tuple-element.6.states_in, f32[1,64]{1,0:T(1,128)S(1)} %get-tuple-element.7.scores_in), custom_call_target="tpu_custom_call" | custom-call | tf_op jit(solution)/shard_map/pallas_call | solution.py:649

commit v3 on v2

--- a/solution.py
+++ b/solution.py
@@ -39,7 +39,7 @@
     def key(block):
         handed_on = 0 <= 2 * at - block < count and relayed(block, 2 * at - block, count)
         hops = at - block if block < at else at + 0.6 * (block - at)
-        return not (handed_on and abs(at - block) == 1), relayed(block, at, count), hops
+        return at <= 1 and block, not (handed_on and abs(at - block) == 1), relayed(block, at, count), hops
 
     return sorted((b for b in range(count) if b != at), key=key)
 
@@ -96,8 +96,6 @@
     q_load,
     above,
     peers,
-    pass_send,
-    pass_user_send,
     q_send,
     q_recv,
     u_send,
@@ -161,7 +159,7 @@
                 (len_hbm, len_ref),
                 (k_hbm, k_buf),
                 (v_hbm, v_buf),
-                (gate_hbm, gate.at[x, c]),
+                (gate_hbm, gate.at[2 * x + c]),
                 (b_hbm.at[:, mine_cols], b_buf),
                 (o_hbm.at[:, mine_cols], o_buf),
                 (w_hbm.at[:, mine_cols], w_buf.at[c]),
@@ -210,13 +208,13 @@
         return remote(
             q_all.at[z, chunk],
             q_all.at[z, chunk],
-            q_send.at[there],
+            q_send,
             q_recv.at[z, chunk],
             {"hist": there},
         )
 
     def user_copy(there):
-        return remote(u_all.at[z], u_all.at[z], u_send.at[there], u_recv.at[z], {"hist": there})
+        return remote(u_all.at[z], u_all.at[z], u_send, u_recv.at[z], {"hist": there})
 
     def send_queries(there):
         user_copy(there).start()
@@ -280,16 +278,21 @@
         user_col = jnp.broadcast_to(u_all[index], (128, rows)).T[:, :1]
         return jnp.where(user_col == owner, 1.0, 0.0).astype(F32)
 
-    def attend(query, live, head):
+    def scored(query, head):
         cols = slice(head * DH, (head + 1) * DH)
-        s = lax.dot_general(
+        return lax.dot_general(
             query,
             k_buf[:, :, cols].reshape(events, DH),
             (((1,), (1,)), ((), ())),
             preferred_element_type=F32,
         )
+
+    def weighed(s, live, head):
         half = s * half_scale + bias[head : head + 1, :]
-        weight = ((half + half * jnp.tanh(half)) * live).astype(BF16)
+        return ((half + half * jnp.tanh(half)) * live).astype(BF16)
+
+    def gathered(weight, head):
+        cols = slice(head * DH, (head + 1) * DH)
         return jnp.dot(
             weight, v_buf[:, :, cols].reshape(events, DH), preferred_element_type=F32
         )
@@ -297,10 +300,10 @@
     per_chunk = heads // chunks
 
     def share_of(block, live, chunk):
-        parts = [
-            attend(q_all[block, chunk, :, i * DH : (i + 1) * DH], live, chunk * per_chunk + i)
-            for i in range(per_chunk)
-        ]
+        mine = [chunk * per_chunk + i for i in range(per_chunk)]
+        s = [scored(q_all[block, chunk, :, i * DH : (i + 1) * DH], head) for i, head in enumerate(mine)]
+        weights = [weighed(s[i], live, head) for i, head in enumerate(mine)]
+        parts = [gathered(weights[i], head) for i, head in enumerate(mine)]
         return jnp.concatenate(parts, axis=1) if per_chunk > 1 else parts[0]
 
     own_live = live_of(z)
@@ -318,29 +321,26 @@
     @pl.when(rank < 2 * n_tower - 1)
     def _():
         pl.semaphore_wait(peers, 2 * n_tower - 1 - rank)
-    sends = []
     w_copy = remote(
         w_hbm.at[:, mate_cols], w_buf.at[c], w_send.at[0], w_recv.at[0], {"head": mate}
     )
     w_copy.start()
-    sends.append(w_copy)
     for i, (t, h) in enumerate(tower_peers):
         copy = remote(
-            gate_hbm, gate.at[x, c], gate_send.at[i], gate_recv.at[x, c], tower_id(t, h)
+            gate_hbm, gate.at[2 * x + c], gate_send, gate_recv.at[2 * x + c], tower_id(t, h)
         )
         copy.start()
-        sends.append(copy)
 
     def user_arrives(block):
         remote(
-            u_all.at[block], u_all.at[block], u_send.at[0], u_recv.at[block], {"hist": block}
+            u_all.at[block], u_all.at[block], u_send, u_recv.at[block], {"hist": block}
         ).wait_recv()
 
     def query_arrives(block, chunk):
         remote(
             q_all.at[block, chunk],
             q_all.at[block, chunk],
-            q_send.at[0],
+            q_send,
             q_recv.at[block, chunk],
             {"hist": block},
         ).wait_recv()
@@ -349,7 +349,7 @@
         return remote(
             q_all.at[block, chunk],
             q_all.at[block, chunk],
-            pass_send.at[step],
+            q_send,
             q_recv.at[block, chunk],
             {"hist": there},
         )
@@ -358,7 +358,7 @@
         return remote(
             u_all.at[block],
             u_all.at[block],
-            pass_user_send.at[step],
+            u_send,
             u_recv.at[block],
             {"hist": there},
         )
@@ -367,7 +367,7 @@
         return remote(
             share_out.at[step, chunk],
             share_in.at[z, chunk],
-            share_send.at[step],
+            share_send,
             share_recv.at[z, chunk],
             {"hist": steps[step][0]},
         )
@@ -414,13 +414,22 @@
 
     sources = [block for block, _, _ in steps]
 
+    def att_copy(tower, head, chunk, device_id):
+        return remote(
+            att_buf.at[2 * tower + head, chunk],
+            att_buf.at[2 * tower + head, chunk],
+            att_send,
+            att_recv.at[2 * tower + head],
+            device_id,
+        )
+
     own = []
     for chunk in range(chunks):
         for src in sources:
             remote(
                 share_out.at[0, chunk],
                 share_in.at[src, chunk],
-                share_send.at[0],
+                share_send,
                 share_recv.at[src, chunk],
                 {"hist": src},
             ).wait_recv()
@@ -428,32 +437,26 @@
         for src in sources:
             part = part + share_in[src, chunk].astype(F32)
         own.append(part)
-        att_buf[x, c, chunk] = part.astype(BF16)
-        for i, (t, h) in reversed(list(enumerate(tower_peers))):
-            copy = remote(
-                att_buf.at[x, c, chunk],
-                att_buf.at[x, c, chunk],
-                att_send.at[i],
-                att_recv.at[x, c, chunk],
-                tower_id(t, h),
-            )
-            copy.start()
+        att_buf[2 * x + c, chunk] = part.astype(BF16)
+        for t in range(1, n_tower):
+            for head in range(2):
+                att_copy(x, c, chunk, {"tower": partner_of(x, t, n_tower), "head": head}).start()
+        att_copy(x, c, chunk, {"head": mate}).start()
 
     def half_arrives(tower, head):
         remote(
-            gate_hbm, gate.at[tower, head], gate_send.at[0], gate_recv.at[tower, head], {"head": mate}
+            gate_hbm, gate.at[2 * tower + head], gate_send, gate_recv.at[2 * tower + head], {"head": mate}
         ).wait_recv()
-        for chunk in range(chunks):
-            remote(
-                att_buf.at[tower, head, chunk],
-                att_buf.at[tower, head, chunk],
-                att_send.at[0],
-                att_recv.at[tower, head, chunk],
-                {"head": mate},
-            ).wait_recv()
+        remote(
+            att_buf.at[2 * tower + head],
+            att_buf.at[2 * tower + head],
+            att_send,
+            att_recv.at[2 * tower + head],
+            {"head": mate},
+        ).wait_recv()
 
     def half_of(tower, head):
-        return [att_buf[tower, head, chunk].astype(F32) for chunk in range(chunks)]
+        return [att_buf[2 * tower + head, chunk].astype(F32) for chunk in range(chunks)]
 
     def normalised(pieces, gates):
         every = [p for half in pieces for p in half]
@@ -484,82 +487,67 @@
         return jnp.sum(acc.T, axis=0, keepdims=True)
 
     half_arrives(x, mate)
-    mine, theirs = normalised([own, half_of(x, mate)], [gate[x, c], gate[x, mate]])
+    mine, theirs = normalised([own, half_of(x, mate)], [gate[2 * x + c], gate[2 * x + mate]])
     states_out[...] = mine
     own_scores = scores_of(mine, c, theirs, mate)
-    score_in[x, c] = own_scores
+    score_in[2 * x + c] = own_scores
     copy = remote(
-        score_in.at[x, c], score_in.at[x, c], score_send_sem.at[0], score_recv.at[x, c], {"head": mate}
+        score_in.at[2 * x + c], score_in.at[2 * x + c], score_send_sem, score_recv.at[2 * x + c], {"head": mate}
     )
     copy.start()
-    sends.append(copy)
     for t in range(1, n_tower):
         other = source_of(x, t, n_tower)
         half_arrives(other, c)
         half_arrives(other, mate)
         first, second = normalised(
-            [half_of(other, 0), half_of(other, 1)], [gate[other, 0], gate[other, 1]]
+            [half_of(other, 0), half_of(other, 1)], [gate[2 * other], gate[2 * other + 1]]
         )
         score_send[t] = scores_of(first, 0, second, 1)
         for h in range(2):
             copy = remote(
                 score_send.at[t],
-                score_in.at[x, c],
-                score_send_sem.at[2 * t + h],
-                score_recv.at[x, c],
-                {"tower": other, "head": mate if h else c},
+                score_in.at[2 * x + c],
+                score_send_sem,
+                score_recv.at[2 * x + c],
+                {"tower": other, "head": h},
             )
             copy.start()
-            sends.append(copy)
 
     for t, h in tower_peers:
         tower, head = partner_of(x, t, n_tower), mate if h else c
         remote(
-            score_in.at[tower, head],
-            score_in.at[tower, head],
-            score_send_sem.at[0],
-            score_recv.at[tower, head],
+            score_in.at[2 * tower + head],
+            score_in.at[2 * tower + head],
+            score_send_sem,
+            score_recv.at[2 * tower + head],
             {"head": mate},
         ).wait_recv()
-    total = score_in[0, 0] + score_in[0, 1]
+    total = score_in[0] + score_in[1]
     for t in range(1, n_tower):
-        total = total + (score_in[t, 0] + score_in[t, 1])
+        total = total + (score_in[2 * t] + score_in[2 * t + 1])
     scores_out[...] = total
-    for copy in sends:
-        copy.wait_send()
-    for i, (t, h) in enumerate(tower_peers):
-        remote(
-            att_buf.at[x, c], att_buf.at[x, c], att_send.at[i], att_recv.at[x, c, 0], tower_id(t, h)
-        ).wait_send()
-    for step, (block, passing, there) in enumerate(steps):
-        remote(
-            share_out.at[step], share_in.at[z], share_send.at[step], share_recv.at[z, 0], {"hist": block}
-        ).wait_send()
-
-        @when(passing)
-        def _():
-            pass_user(step, block, there).wait_send()
-            remote(
-                q_all.at[block], q_all.at[block], pass_send.at[step], q_recv.at[block, 0], {"hist": there}
-            ).wait_send()
-
-    def sent(there):
-        user_copy(there).wait_send()
-        remote(
-            q_all.at[z], q_all.at[z], q_send.at[there], q_recv.at[z, 0], {"hist": there}
-        ).wait_send()
-
-    for distance in range(1, n_hist):
-        for sign, exists in ((-1, z >= distance), (1, z + distance < n_hist)):
-
-            @pl.when(exists)
-            def _(distance=distance, sign=sign):
-                when(goes_direct(distance, sign))(lambda: sent(z + sign * distance))
-
-
-def hand_over(states_in, scores_in, states_out, scores_out):
-    states_out[...] = states_in[...]
-    scores_out[...] = scores_in[...]
+    w_copy.wait_send()
+    others, peer_count = slice(0, n_hist - 1), slice(0, 2 * n_tower - 1)
+    for ref, send, recv in (
+        (q_all.at[others], q_send, q_recv.at[0, 0]),
+        (u_all.at[others], u_send, u_recv.at[0]),
+        (share_out.at[others], share_send, share_recv.at[0, 0]),
+        (gate.at[peer_count], gate_send, gate_recv.at[0]),
+        (att_buf.at[peer_count], att_send, att_recv.at[0]),
+        (score_in.at[peer_count], score_send_sem, score_recv.at[0]),
+    ):
+        remote(ref, ref, send, recv, {"head": mate}).wait_send()
+
+
+def hand_over(states_in, scores_in, states_out, scores_out, sems):
+    copies = [
+        pltpu.make_async_copy(states_in, states_out, sems.at[0]),
+        pltpu.make_async_copy(scores_in, scores_out, sems.at[1]),
+    ]
+    for copy in copies:
+        copy.start()
+    for copy in copies:
+        copy.wait()
 
 
 def local(
@@ -600,7 +588,7 @@
             pltpu.VMEM(hist_values.shape, BF16),
             pltpu.VMEM(time_bucket.shape, jnp.int32),
             pltpu.VMEM((1,) + hist_len.shape, jnp.int32),
-            pltpu.VMEM((n_tower, 2, rows, feat), BF16),
+            pltpu.VMEM((2 * n_tower, rows, feat), BF16),
             pltpu.VMEM(time_bias.shape[::-1], F32),
             pltpu.VMEM((2, feat, hidden), BF16),
             pltpu.VMEM((1, hidden), F32),
@@ -608,29 +596,27 @@
             pltpu.VMEM((chunks, rows, width), F32),
             pltpu.VMEM((n_hist, chunks, rows, width), BF16),
             pltpu.VMEM((n_hist, chunks, rows, width), BF16),
-            pltpu.VMEM((n_tower, 2, chunks, rows, width), BF16),
+            pltpu.VMEM((2 * n_tower, chunks, rows, width), BF16),
             pltpu.VMEM((n_tower, 1, rows), F32),
-            pltpu.VMEM((n_tower, 2, 1, rows), F32),
+            pltpu.VMEM((2 * n_tower, 1, rows), F32),
             dma((10,)),
             dma,
             pltpu.SemaphoreType.REGULAR((n_hist,)),
             pltpu.SemaphoreType.REGULAR,
-            dma((n_hist - 1,)),
-            dma((n_hist - 1,)),
+            dma,
+            dma((n_hist, chunks)),
+            dma,
             dma((n_hist,)),
-            dma((n_hist, chunks)),
-            dma((n_hist,)),
-            dma((n_hist,)),
-            dma((n_hist - 1,)),
+            dma,
             dma((n_hist, chunks)),
             dma((1,)),
             dma((1,)),
-            dma((2 * n_tower - 1,)),
-            dma((n_tower, 2)),
-            dma((2 * n_tower - 1,)),
-            dma((n_tower, 2, chunks)),
+            dma,
             dma((2 * n_tower,)),
-            dma((n_tower, 2)),
+            dma,
+            dma((2 * n_tower,)),
+            dma,
+            dma((2 * n_tower,)),
         ],
         compiler_params=pltpu.CompilerParams(collective_id=0, has_side_effects=True),
     )(
@@ -653,7 +639,8 @@
             jax.ShapeDtypeStruct((1, rows), F32),
         ),
         in_specs=[vmem_spec, vmem_spec],
-        out_specs=(vmem_spec, vmem_spec),
+        out_specs=(any_spec, any_spec),
+        scratch_shapes=[dma((2,))],
     )(
         pltpu.with_memory_space_constraint(states, pltpu.VMEM),
         pltpu.with_memory_space_constraint(scores, pltpu.VMEM),

time: 25.6 us -> 24.8 us (0.969)
  Pallas kernels: 24.8 us -> 24 us
    pallas_call x1, Pallas kernels: 24.1 us -> 23.4 us  [local(): pl.pallas_call(functools.partial(kernel, n_hist, n_tower), out_shape=(plt...]
where the time goes in v3:
time: 24.8 us; the launch traced here: 24.7 us
  Pallas kernels  24 us (97%)
  between operations  0.64 us (3%)
    pallas_call x1, Pallas kernels, local(): pl.pallas_call(functools.partial(kernel, n_hist, n_tower), out_shape=(plt...  23.4 us
    pallas_call x1, Pallas kernels, local(): pl.pallas_call(hand_over, out_shape=(jax.ShapeDtypeStruct((rows, feat), B...  0.65 us

profile of v3, /device:TPU:0, one launch (start us, length us, event | category | flops | bytes accessed | tf_op | source)
XLA Modules:
  0.0 24.7 jit_solution(14624299670708586748)
XLA Ops:
  0.6 23.4 %shard_map.122 = (bf16[64,512]{1,0:T(8,128)(2,1)S(1)}, f32[1,64]{1,0:T(1,128)S(1)}) custom-call(bf16[64,512]{1,0:T(8,128)(2,1)} %q_hbm.1, bf16[2,256,512]{2,1,0:T(8,128)(2,1)} %k_hbm.1, bf16[2,256,512]{2,1,0:T(8,128)(2,1)} %v_hbm.1, s32[1,64]{1,0:T(1,128)} %bitcast.9, s32[2,256]{1,0:T(2,128)} %bucket_hbm.1, s32[1,2]{1,0:T(1,128)} %bitcast.10, ...), custom_call_target="tpu_custom_call" | custom-call | tf_op jit(solution)/shard_map/pallas_call | solution.py:576
  24.0 0.7 %shard_map.123 = (bf16[64,512]{1,0:T(8,128)(2,1)}, f32[1,64]{1,0:T(1,128)}) custom-call(bf16[64,512]{1,0:T(8,128)(2,1)S(1)} %get-tuple-element.6.states_in, f32[1,64]{1,0:T(1,128)S(1)} %get-tuple-element.7.scores_in), custom_call_target="tpu_custom_call" | custom-call | tf_op jit(solution)/shard_map/pallas_call | solution.py:635

commit v4 on v3

--- a/solution.py
+++ b/solution.py
@@ -31,15 +31,21 @@
     return partner_of(me, step, count)
 
 
-def relayed(block, at, count):
-    return abs(block - at) == 2 and block not in (0, count - 1)
-
-
-def order_of(at, count):
+def relayed(block, at, count, core):
+    gap, from_end = abs(block - at), block in (0, count - 1)
+    return gap == 2 and not from_end or core == 1 and gap == 3 and from_end
+
+
+def handed_on(block, at, count, core):
+    there = at + (1 if at > block else -1)
+    return there if 0 <= there < count and relayed(block, there, count, core) else None
+
+
+def order_of(at, count, core):
     def key(block):
-        handed_on = 0 <= 2 * at - block < count and relayed(block, 2 * at - block, count)
         hops = at - block if block < at else at + 0.6 * (block - at)
-        return at <= 1 and block, not (handed_on and abs(at - block) == 1), relayed(block, at, count), hops
+        passed = handed_on(block, at, count, core) is not None
+        return not passed, relayed(block, at, count, core), hops
 
     return sorted((b for b in range(count) if b != at), key=key)
 
@@ -135,13 +141,19 @@
         (t, h, rank_of(partner_of(x, t, n_tower), mate if h else c)) for t, h in tower_peers
     ]
     barrier = pltpu.get_barrier_semaphore()
+    for distance in range(1, n_hist):
+
+        @pl.when(z + distance < n_hist)
+        def _(distance=distance):
+            pl.semaphore_signal(
+                barrier, inc=1, device_id={"hist": z + distance}, device_id_type=MESH
+            )
+
     for t, h, other_rank in peer_ranks:
 
         @pl.when(other_rank > rank)
         def _(t=t, h=h):
             pl.semaphore_signal(barrier, inc=1, device_id=tower_id(t, h), device_id_type=MESH)
-
-    has_left, has_right = z > 0, z < n_hist - 1
 
     mine_cols = pl.ds(pl.multiple_of(c * hidden, 128), hidden)
     mate_cols = pl.ds(pl.multiple_of(mate * hidden, 128), hidden)
@@ -170,15 +182,11 @@
     for load in q_loads + loads[:6]:
         load.start()
 
-    awaited = rank + has_left.astype(jnp.int32)
+    awaited = rank + z
 
     @pl.when(awaited > 0)
     def _():
         pl.semaphore_wait(barrier, awaited)
-
-    @pl.when(has_right)
-    def _():
-        pl.semaphore_signal(barrier, inc=1, device_id={"hist": z + 1}, device_id_type=MESH)
 
     for distance in range(1, n_hist):
 
@@ -221,10 +229,22 @@
         for chunk in range(chunks):
             query_copy(there, chunk).start()
 
+    places = [(at, core) for at in range(n_hist) for core in range(2)]
+    place = 2 * z + c
+
+    def flag(values):
+        chosen = pick(place, [int(v) for v in values])
+        return bool(chosen) if isinstance(chosen, int) else chosen == 1
+
     def goes_direct(distance, sign):
-        if distance != 2:
-            return True
-        return z == 0 if sign > 0 else z == n_hist - 1
+        return flag(
+            [
+                not relayed(at, at + sign * distance, n_hist, core)
+                if 0 <= at + sign * distance < n_hist
+                else False
+                for at, core in places
+            ]
+        )
 
     def send_down(distance):
         @pl.when(z >= distance)
@@ -372,21 +392,18 @@
             {"hist": steps[step][0]},
         )
 
-    def flag(values):
-        chosen = pick(z, [int(v) for v in values])
-        return bool(chosen) if isinstance(chosen, int) else chosen == 1
-
-    orders = [order_of(i, n_hist) for i in range(n_hist)]
+    orders = [order_of(at, n_hist, core) for at, core in places]
     steps = []
     for step in range(n_hist - 1):
         blocks = [order[step] for order in orders]
-        onward = [2 * i - b for i, b in enumerate(blocks)]
-        hands_on = [
-            abs(i - b) == 1 and 0 <= e < n_hist and relayed(b, e, n_hist)
-            for i, (b, e) in enumerate(zip(blocks, onward))
-        ]
-        targets = [e if on else 0 for e, on in zip(onward, hands_on)]
-        steps.append((pick(z, blocks), flag(hands_on), pick(z, targets)))
+        targets = [handed_on(b, at, n_hist, core) for b, (at, core) in zip(blocks, places)]
+        steps.append(
+            (
+                pick(place, blocks),
+                flag([there is not None for there in targets]),
+                pick(place, [there or 0 for there in targets]),
+            )
+        )
 
     for step, (block, passing, there) in enumerate(steps):
         user_arrives(block)
@@ -527,10 +544,26 @@
         total = total + (score_in[2 * t] + score_in[2 * t + 1])
     scores_out[...] = total
     w_copy.wait_send()
+    sent = [
+        sum(
+            (not relayed(at, b, n_hist, core)) + (handed_on(b, at, n_hist, core) is not None)
+            for b in range(n_hist)
+            if b != at
+        )
+        for at, core in places
+    ]
+    for count in sorted(set(sent)):
+
+        @when(flag([n == count for n in sent]))
+        def _(count=count):
+            for ref, send, recv in (
+                (q_all.at[0:count], q_send, q_recv.at[0, 0]),
+                (u_all.at[0:count], u_send, u_recv.at[0]),
+            ):
+                remote(ref, ref, send, recv, {"head": mate}).wait_send()
+
     others, peer_count = slice(0, n_hist - 1), slice(0, 2 * n_tower - 1)
     for ref, send, recv in (
-        (q_all.at[others], q_send, q_recv.at[0, 0]),
-        (u_all.at[others], u_send, u_recv.at[0]),
         (share_out.at[others], share_send, share_recv.at[0, 0]),
         (gate.at[peer_count], gate_send, gate_recv.at[0]),
         (att_buf.at[peer_count], att_send, att_recv.at[0]),

time: 24.8 us -> 23.7 us (0.956); the launches traced: 24.7 us -> 23.3 us
  Pallas kernels: 24 us -> 22.6 us
    pallas_call x1, Pallas kernels: 23.4 us -> 22 us  [local(): pl.pallas_call(functools.partial(kernel, n_hist, n_tower), out_shape=(plt...]
where the time goes in v4:
time: 23.7 us; the launch traced here: 23.3 us
  Pallas kernels  22.6 us (95%)
  between operations  0.64 us (3%)
    pallas_call x1, Pallas kernels, local(): pl.pallas_call(functools.partial(kernel, n_hist, n_tower), out_shape=(plt...  22 us
    pallas_call x1, Pallas kernels, local(): pl.pallas_call(hand_over, out_shape=(jax.ShapeDtypeStruct((rows, feat), B...  0.65 us

profile of v4, /device:TPU:0, one launch (start us, length us, event | category | flops | bytes accessed | tf_op | source)
XLA Modules:
  0.0 23.3 jit_solution(2873534788390602950)
XLA Ops:
  0.6 22.0 %shard_map.122 = (bf16[64,512]{1,0:T(8,128)(2,1)S(1)}, f32[1,64]{1,0:T(1,128)S(1)}) custom-call(bf16[64,512]{1,0:T(8,128)(2,1)} %q_hbm.1, bf16[2,256,512]{2,1,0:T(8,128)(2,1)} %k_hbm.1, bf16[2,256,512]{2,1,0:T(8,128)(2,1)} %v_hbm.1, s32[1,64]{1,0:T(1,128)} %bitcast.9, s32[2,256]{1,0:T(2,128)} %bucket_hbm.1, s32[1,2]{1,0:T(1,128)} %bitcast.10, ...), custom_call_target="tpu_custom_call" | custom-call | tf_op jit(solution)/shard_map/pallas_call | solution.py:609
  22.6 0.7 %shard_map.123 = (bf16[64,512]{1,0:T(8,128)(2,1)}, f32[1,64]{1,0:T(1,128)}) custom-call(bf16[64,512]{1,0:T(8,128)(2,1)S(1)} %get-tuple-element.6.states_in, f32[1,64]{1,0:T(1,128)S(1)} %get-tuple-element.7.scores_in), custom_call_target="tpu_custom_call" | custom-call | tf_op jit(solution)/shard_map/pallas_call | solution.py:668

commit v5 on v4

--- a/solution.py
+++ b/solution.py
@@ -43,8 +43,10 @@
 
 def order_of(at, count, core):
     def key(block):
+        passed = handed_on(block, at, count, core) is not None
+        if 2 * at < count:
+            return core == 0 and not passed, block
         hops = at - block if block < at else at + 0.6 * (block - at)
-        passed = handed_on(block, at, count, core) is not None
         return not passed, relayed(block, at, count, core), hops
 
     return sorted((b for b in range(count) if b != at), key=key)

time: 23.7 us -> 23.2 us (0.979); the launches traced: 23.3 us -> 23 us
    pallas_call x1, Pallas kernels: 22 us -> 21.8 us  [local(): pl.pallas_call(functools.partial(kernel, n_hist, n_tower), out_shape=(plt...]
where the time goes in v5:
time: 23.2 us; the launch traced here: 23 us
  Pallas kernels  22.4 us (97%)
  between operations  0.64 us (3%)
    pallas_call x1, Pallas kernels, local(): pl.pallas_call(functools.partial(kernel, n_hist, n_tower), out_shape=(plt...  21.8 us
    pallas_call x1, Pallas kernels, local(): pl.pallas_call(hand_over, out_shape=(jax.ShapeDtypeStruct((rows, feat), B...  0.65 us

profile of v5, /device:TPU:0, one launch (start us, length us, event | category | flops | bytes accessed | tf_op | source)
XLA Modules:
  0.0 23.0 jit_solution(7791111640385545596)
XLA Ops:
  0.6 21.8 %shard_map.122 = (bf16[64,512]{1,0:T(8,128)(2,1)S(1)}, f32[1,64]{1,0:T(1,128)S(1)}) custom-call(bf16[64,512]{1,0:T(8,128)(2,1)} %q_hbm.1, bf16[2,256,512]{2,1,0:T(8,128)(2,1)} %k_hbm.1, bf16[2,256,512]{2,1,0:T(8,128)(2,1)} %v_hbm.1, s32[1,64]{1,0:T(1,128)} %bitcast.9, s32[2,256]{1,0:T(2,128)} %bucket_hbm.1, s32[1,2]{1,0:T(1,128)} %bitcast.10, ...), custom_call_target="tpu_custom_call" | custom-call | tf_op jit(solution)/shard_map/pallas_call | solution.py:611
  22.4 0.7 %shard_map.123 = (bf16[64,512]{1,0:T(8,128)(2,1)}, f32[1,64]{1,0:T(1,128)}) custom-call(bf16[64,512]{1,0:T(8,128)(2,1)S(1)} %get-tuple-element.6.states_in, f32[1,64]{1,0:T(1,128)S(1)} %get-tuple-element.7.scores_in), custom_call_target="tpu_custom_call" | custom-call | tf_op jit(solution)/shard_map/pallas_call | solution.py:670

commit v6 on v5

--- a/solution.py
+++ b/solution.py
@@ -195,7 +195,7 @@
         @pl.when(z >= distance)
         def _(distance=distance):
             pl.semaphore_signal(
-                above.at[z], inc=1, device_id={"hist": z - distance}, device_id_type=MESH
+                above.at[z - 1], inc=1, device_id={"hist": z - distance}, device_id_type=MESH
             )
 
     for t, h, other_rank in peer_ranks:
@@ -214,17 +214,20 @@
             device_id_type=MESH,
         )
 
+    def slot_of(block, at):
+        return lax.rem(block - at + n_hist, n_hist) - 1
+
     def query_copy(there, chunk):
         return remote(
             q_all.at[z, chunk],
             q_all.at[z, chunk],
             q_send,
-            q_recv.at[z, chunk],
+            q_recv.at[slot_of(z, there), chunk],
             {"hist": there},
         )
 
     def user_copy(there):
-        return remote(u_all.at[z], u_all.at[z], u_send, u_recv.at[z], {"hist": there})
+        return remote(u_all.at[z], u_all.at[z], u_send, u_recv.at[slot_of(z, there)], {"hist": there})
 
     def send_queries(there):
         user_copy(there).start()
@@ -256,7 +259,7 @@
     def send_up(distance, condition):
         @pl.when(condition)
         def _():
-            pl.semaphore_wait(above.at[z + distance], 1)
+            pl.semaphore_wait(above.at[z + distance - 1], 1)
             when(goes_direct(distance, 1))(lambda: send_queries(z + distance))
 
     user_load.wait()
@@ -355,7 +358,7 @@
 
     def user_arrives(block):
         remote(
-            u_all.at[block], u_all.at[block], u_send, u_recv.at[block], {"hist": block}
+            u_all.at[block], u_all.at[block], u_send, u_recv.at[slot_of(block, z)], {"hist": block}
         ).wait_recv()
 
     def query_arrives(block, chunk):
@@ -363,7 +366,7 @@
             q_all.at[block, chunk],
             q_all.at[block, chunk],
             q_send,
-            q_recv.at[block, chunk],
+            q_recv.at[slot_of(block, z), chunk],
             {"hist": block},
         ).wait_recv()
 
@@ -372,7 +375,7 @@
             q_all.at[block, chunk],
             q_all.at[block, chunk],
             q_send,
-            q_recv.at[block, chunk],
+            q_recv.at[slot_of(block, there), chunk],
             {"hist": there},
         )
 
@@ -381,7 +384,7 @@
             u_all.at[block],
             u_all.at[block],
             u_send,
-            u_recv.at[block],
+            u_recv.at[slot_of(block, there)],
             {"hist": there},
         )
 
@@ -390,7 +393,7 @@
             share_out.at[step, chunk],
             share_in.at[z, chunk],
             share_send,
-            share_recv.at[z, chunk],
+            share_recv.at[slot_of(z, steps[step][0]), chunk],
             {"hist": steps[step][0]},
         )
 
@@ -449,7 +452,7 @@
                 share_out.at[0, chunk],
                 share_in.at[src, chunk],
                 share_send,
-                share_recv.at[src, chunk],
+                share_recv.at[slot_of(src, z), chunk],
                 {"hist": src},
             ).wait_recv()
         part = own_share[chunk]
@@ -636,14 +639,14 @@
             pltpu.VMEM((2 * n_tower, 1, rows), F32),
             dma((10,)),
             dma,
-            pltpu.SemaphoreType.REGULAR((n_hist,)),
+            pltpu.SemaphoreType.REGULAR((n_hist - 1,)),
             pltpu.SemaphoreType.REGULAR,
             dma,
-            dma((n_hist, chunks)),
+            dma((n_hist - 1, chunks)),
             dma,
-            dma((n_hist,)),
+            dma((n_hist - 1,)),
             dma,
-            dma((n_hist, chunks)),
+            dma((n_hist - 1, chunks)),
             dma((1,)),
             dma((1,)),
             dma,

time: 23.2 us -> 23.2 us (level)
  no operation moved by 1% of the time
where the time goes in v6:
time: 23.2 us; the launch traced here: 23 us
  Pallas kernels  22.4 us (97%)
  between operations  0.64 us (3%)
    pallas_call x1, Pallas kernels, local(): pl.pallas_call(functools.partial(kernel, n_hist, n_tower), out_shape=(plt...  21.7 us
    pallas_call x1, Pallas kernels, local(): pl.pallas_call(hand_over, out_shape=(jax.ShapeDtypeStruct((rows, feat), B...  0.65 us

profile of v6, /device:TPU:0, one launch (start us, length us, event | category | flops | bytes accessed | tf_op | source)
XLA Modules:
  0.0 23.0 jit_solution(9895851910627982360)
XLA Ops:
  0.6 21.7 %shard_map.122 = (bf16[64,512]{1,0:T(8,128)(2,1)S(1)}, f32[1,64]{1,0:T(1,128)S(1)}) custom-call(bf16[64,512]{1,0:T(8,128)(2,1)} %q_hbm.1, bf16[2,256,512]{2,1,0:T(8,128)(2,1)} %k_hbm.1, bf16[2,256,512]{2,1,0:T(8,128)(2,1)} %v_hbm.1, s32[1,64]{1,0:T(1,128)} %bitcast.9, s32[2,256]{1,0:T(2,128)} %bucket_hbm.1, s32[1,2]{1,0:T(1,128)} %bitcast.10, ...), custom_call_target="tpu_custom_call" | custom-call | tf_op jit(solution)/shard_map/pallas_call | solution.py:614
  22.4 0.7 %shard_map.123 = (bf16[64,512]{1,0:T(8,128)(2,1)}, f32[1,64]{1,0:T(1,128)}) custom-call(bf16[64,512]{1,0:T(8,128)(2,1)S(1)} %get-tuple-element.6.states_in, f32[1,64]{1,0:T(1,128)S(1)} %get-tuple-element.7.scores_in), custom_call_target="tpu_custom_call" | custom-call | tf_op jit(solution)/shard_map/pallas_call | solution.py:673
